TPU v7x, 128 devices: a whole 4x4x4 slice. The times are simulated.
128 devices in a mesh: leaf: 4 (over y), row: 8 (over z, core), col: 4 (over x).
Axes of the slice: x: 4, y: 4, z: 4, core: 2. Of those that a mesh axis runs over, the one named last changes fastest.
Arguments:
- sigma_top: float32 [1024, 1024], P(('leaf', 'row'), 'col')
- panels: float32 [4, 7, 1024, 512], P('leaf', None, 'row', 'col'), may hold values from -0.1875 to 0.1875
- inverse_diag: float32 [4, 7, 512, 512], P('leaf', None, 'col')
- slot_lists: int32 [4, 6, 8], P('leaf'), may hold values from -1 to 11, as said below
- parent_links: int32 [4, 4], P('leaf'), may hold values from 1 to 2
Outputs:
- ancestor_block: float32 [4, 7, 1024, 512], P('leaf', None, 'row', 'col')
- diagonal_block: float32 [4, 7, 512, 512], P('leaf', None, None, 'col')
Inputs may be any that keep to these rules, and one draw needn't show every extreme that they name: `slot_lists`: in every row, entries 0 to 3 are 8 to 11 in order (the parent's own tiles); then come 1 to 3 distinct parent ancestor slots, below 8 for supernodes 1 and 2 and below 4 for supernodes 3 to 6; the rest are -1, so every row has padding. `parent_links`: each supernode 3 to 6 has supernode 1 or 2 as its parent. `sigma_top`: symmetric.
All inputs are finite; a program needn't handle non-finite values.
Results may differ from a plain program's by a relative error of at most 0.0001.
Values sent between devices are 32-bit elements; how exact they have to be, the bound alone decides.
A program may use at most 128 MiB of HBM per device.

v0:
```python
import jax
import jax.numpy as jnp
from jax import lax
from jax.sharding import PartitionSpec as P

TILE = 128
HIGHEST = lax.Precision.HIGHEST


def mm(a, b):
    return jnp.matmul(a, b, precision=HIGHEST, preferred_element_type=jnp.float32)


def tile_rows(matrix, index, tile):
    return lax.dynamic_slice_in_dim(matrix, index * tile, tile, 0)


def tile_cols(matrix, index, tile):
    return lax.dynamic_slice_in_dim(matrix, index * tile, tile, 1)


def scatter_factor(factor_col, slots, positions, tile):
    tiles = factor_col.reshape(slots.shape[0], tile, factor_col.shape[1])
    hits = slots[:, None] == jnp.arange(positions, dtype=slots.dtype)[None, :]
    present = jnp.any(hits, axis=0)
    source = jnp.argmax(hits, axis=0)
    moved = jnp.take(tiles, source, axis=0)
    moved = jnp.where(present[:, None, None], moved, 0.0)
    return moved.reshape(positions * tile, factor_col.shape[1])


def body(sigma_top, panels, inverse_diag, slot_lists, parent_links):
    tile = TILE
    row_count = lax.axis_size("row")
    col_count = lax.axis_size("col")
    leaf_count = lax.axis_size("leaf")
    r = lax.axis_index("row")
    c = lax.axis_index("col")
    panel = panels[0]
    inverse = inverse_diag[0]
    picks_all = slot_lists[0]
    parents = parent_links[0]
    nodes = panel.shape[0]
    width = inverse.shape[2]
    own_tiles = width // tile
    slot_count = picks_all.shape[1]
    positions = slot_count + own_tiles
    band = width // row_count
    partial_factor = mm(panel, inverse)
    factor_rows = lax.psum(partial_factor, "col")
    living = jnp.concatenate([jnp.ones((1, slot_count), jnp.bool_), picks_all >= 0], axis=0)
    live_here = jnp.take(living, r, axis=1).astype(jnp.float32)
    factor_rows = factor_rows * live_here[:, None, None]
    factor_tile = lax.dynamic_slice_in_dim(factor_rows, c * tile, tile, 2)
    factor_cols = lax.all_gather(factor_tile, "row", axis=1, tiled=True)
    inverse_band = lax.dynamic_slice_in_dim(inverse, r * band, band, 2)
    partial_gram = mm(jnp.transpose(inverse_band, (0, 2, 1)), inverse)
    gram_piece = lax.psum_scatter(partial_gram, "col", scatter_dimension=2, tiled=True)
    local_rows, local_cols = sigma_top.shape
    gathered = lax.all_gather(sigma_top, ("leaf", "row", "col"), axis=0)
    sigma = gathered.reshape(leaf_count * row_count, col_count, local_rows, local_cols)
    sigma = jnp.transpose(sigma, (0, 2, 1, 3)).reshape(
        leaf_count * row_count * local_rows, col_count * local_cols
    )

    def diag_partial(first, products):
        rows = factor_rows[first : first + products.shape[0]]
        return mm(jnp.transpose(rows, (0, 2, 1)), products)

    def reduce_and_gather(first, products):
        count = products.shape[0]
        piece = lax.psum_scatter(
            diag_partial(first, products), "row", scatter_dimension=1, tiled=True
        )
        piece = piece + gram_piece[first : first + count]
        both = jnp.concatenate([products, piece], axis=1)
        everything = lax.all_gather(both, ("row", "col"), axis=0)
        return everything.reshape(row_count, col_count, count, tile + band, tile)

    bands_per_tile = tile // band

    def product_col_t(gathered, node, m):
        tiles = lax.dynamic_index_in_dim(gathered[:, :, :, :tile], m, 1, keepdims=False)
        tiles = lax.dynamic_index_in_dim(tiles, node, 1, keepdims=False)
        return jnp.transpose(tiles, (2, 0, 1)).reshape(tile, -1)

    def product_row(gathered, node, q):
        tiles = lax.dynamic_index_in_dim(gathered[:, :, :, :tile], q, 0, keepdims=False)
        tiles = lax.dynamic_index_in_dim(tiles, node, 1, keepdims=False)
        return jnp.transpose(tiles, (1, 0, 2)).reshape(tile, -1)

    def diag_row(gathered, node, m):
        pieces = lax.dynamic_slice_in_dim(
            gathered[:, :, :, tile:], m * bands_per_tile, bands_per_tile, 0
        )
        pieces = lax.dynamic_index_in_dim(pieces, node, 2, keepdims=False)
        return jnp.transpose(pieces, (0, 2, 1, 3)).reshape(tile, -1)

    def diag_col(gathered, m):
        pieces = lax.dynamic_index_in_dim(gathered[:, :, :, tile:], m, 1, keepdims=False)
        return jnp.transpose(pieces, (1, 0, 2, 3)).reshape(pieces.shape[1], -1, tile)

    own_row = jnp.minimum(r, own_tiles - 1)
    upper = r < own_tiles
    product_0 = mm(tile_rows(sigma, r, tile), factor_cols[0])
    gathered_0 = reduce_and_gather(0, product_0[None])
    top_row_1 = jnp.concatenate(
        [-product_col_t(gathered_0, 0, own_row), diag_row(gathered_0, 0, own_row)], axis=1
    )
    level_1 = []
    for node in (1, 2):
        slots = picks_all[node - 1]
        spread = scatter_factor(factor_cols[node], slots, positions, tile)
        source = slots[jnp.maximum(r, own_tiles)]
        source_row = jnp.maximum(source, 0)
        low_row = jnp.concatenate(
            [tile_rows(sigma, source_row, tile), -product_row(gathered_0, 0, source_row)], axis=1
        )
        low_row = jnp.where(source >= 0, low_row, 0.0)
        row = jnp.where(upper, top_row_1, low_row)
        level_1.append(mm(row, spread))
    product_1 = jnp.stack(level_1)
    gathered_1 = reduce_and_gather(1, product_1)
    level_2 = []
    for node in range(3, nodes):
        slots = picks_all[node - 1]
        parent = parents[node - 3] - 1
        parent_slots = jnp.take(picks_all, parent, axis=0)
        spread = scatter_factor(factor_cols[node], slots, positions, tile)
        top_row = jnp.concatenate(
            [-product_col_t(gathered_1, parent, own_row), diag_row(gathered_1, parent, own_row)],
            axis=1,
        )
        source = slots[jnp.maximum(r, own_tiles)]
        source_row = jnp.clip(source, 0, own_tiles - 1)
        corner_tiles = product_col_t(gathered_0, 0, source_row).reshape(tile, slot_count, tile)
        corner_picks = parent_slots[own_tiles:]
        corner = jnp.take(corner_tiles, jnp.maximum(corner_picks, 0), axis=1)
        corner = jnp.where((corner_picks >= 0)[None, :, None], -corner, 0.0).reshape(tile, -1)
        low_row = jnp.concatenate(
            [
                diag_row(gathered_0, 0, source_row),
                corner,
                -product_row(gathered_1, parent, source_row),
            ],
            axis=1,
        )
        low_row = jnp.where(source >= 0, low_row, 0.0)
        row = jnp.where(upper, top_row, low_row)
        level_2.append(mm(row, spread))
    product_2 = jnp.stack(level_2)
    first_2 = 3
    count_2 = product_2.shape[0]
    gram_rows = jnp.zeros((count_2, width, tile), jnp.float32)
    gram_rows = lax.dynamic_update_slice_in_dim(
        gram_rows, gram_piece[first_2 : first_2 + count_2], r * band, 1
    )
    diag_2 = lax.psum(diag_partial(first_2, product_2) + gram_rows, "row")
    products = jnp.concatenate([product_0[None], product_1, product_2], axis=0)
    diag_cols = jnp.concatenate([diag_col(gathered_0, c), diag_col(gathered_1, c), diag_2], axis=0)
    return ((-products)[None], diag_cols[None])


def solution(mesh):
    return jax.shard_map(
        body,
        mesh=mesh,
        in_specs=(
            P(("leaf", "row"), "col"),
            P("leaf", None, "row", "col"),
            P("leaf", None, "col", None),
            P("leaf", None, None),
            P("leaf", None),
        ),
        out_specs=(P("leaf", None, "row", "col"), P("leaf", None, None, "col")),
        check_vma=False,
    )
```

profile of v0, /device:TPU:0, one launch (start us, length us, event | category | flops | bytes accessed | tf_op | source)
XLA Modules:
  0.0 443.9 jit_solution(9169907735359701775)
XLA Ops:
  9.5 3.9 fusion.2
  14.3 57.6 %all-reduce.4.cloned.1.call-done = f32[7,128,512]{2,1,0:T(8,128)} async-done(((f32[7,128,512]{2,1,0:T(8,128)}), f32[7,128,512]{2,1,0:T(8,128)}) %all-reduce.4.cloned.1.call-update) | async-done | bytes 1835024 | tf_op jit(solution)/shard_map/psum | solution.py:50
  75.9 2.3 fusion
  78.3 18.1 %all-gather.10.cloned.1.call-done = f32[4096,256]{1,0:T(8,128)} async-done(((f32[32,256]{1,0:T(8,128)}), f32[4096,256]{1,0:T(8,128)}) %all-gather.10.cloned.1.call-update) | async-done | bytes 4194320 | tf_op jit(solution)/shard_map/all_gather | solution.py:60
  96.3 5.8 %copy.183 = f32[32,4,32,256]{3,1,2,0:T(4,128)S(1)} copy(f32[32,4,32,256]{3,2,1,0:T(8,128)} %bitcast.299) | data formatting | bytes 8388608 | tf_op jit(solution)/shard_map/reshape | solution.py:61
  102.2 3.0 copy.234
  105.1 20.2 %all-gather.8.cloned.1.call-done = f32[7,1024,128]{2,1,0:T(8,128)} async-done(((f32[7,128,128]{2,1,0:T(8,128)}), f32[7,1024,128]{2,1,0:T(8,128)}) %all-gather.8.cloned.1.call-update) | async-done | bytes 3670032 | tf_op jit(solution)/shard_map/all_gather | solution.py:55
  125.3 2.5 bitcast_dynamic-update-slice_fusion.6
  129.2 30.5 %reduce-scatter.4.cloned.1.call-done = f32[1,64,128]{2,1,0:T(8,128)} async-done(((f32[1,512,128]{2,1,0:T(8,128)}), f32[1,64,128]{2,1,0:T(8,128)}) %reduce-scatter.4.cloned.1.call-update) | async-done | bytes 32784 | tf_op jit(solution)/shard_map/reduce_scatter | solution.py:72
  170.7 3.1 fusion.109
  173.7 2.5 gather_fusion.1
  177.7 2.3 select_select_fusion.4
  181.0 2.3 constant_dynamic-slice_fusion.14
  183.3 22.6 %all-gather.12.cloned.1.call-done = f32[32,192,128]{2,1,0:T(8,128)} async-done(((f32[1,192,128]{2,1,0:T(8,128)}), f32[32,192,128]{2,1,0:T(8,128)}) %all-gather.12.cloned.1.call-update) | async-done | bytes 3145744 | tf_op jit(solution)/shard_map/all_gather | solution.py:77
  207.3 2.1 slice.193
  216.4 3.2 constant_dynamic-slice_fusion.6
  220.9 3.1 bitcast_dynamic-update-slice_fusion.5
  227.5 30.5 %reduce-scatter.8.cloned.1.call-done = f32[2,64,128]{2,1,0:T(8,128)} async-done(((f32[2,512,128]{2,1,0:T(8,128)}), f32[2,64,128]{2,1,0:T(8,128)}) %reduce-scatter.8.cloned.1.call-update) | async-done | bytes 65552 | tf_op jit(solution)/shard_map/reduce_scatter | solution.py:72
  273.0 2.5 gather_fusion.7
  289.5 2.3 gather_fusion.8
  299.2 2.3 gather_fusion.6
  306.9 2.1 copy.203
  309.0 2.3 gather_fusion.4
  316.7 2.1 copy.195
  318.8 2.3 gather_fusion.2
  328.1 3.2 slice.198
  336.7 2.1 copy.232
  338.8 2.1 copy.231
  340.9 2.2 negate_bitcast_fusion
  361.5 3.3 bitcast_dynamic-update-slice_fusion.3
  375.5 58.1 %all-reduce.6.cloned.1.call-done = f32[4,512,128]{2,1,0:T(8,128)} async-done(((f32[4,512,128]{2,1,0:T(8,128)}), f32[4,512,128]{2,1,0:T(8,128)}) %all-reduce.6.cloned.1.call-update) | async-done | bytes 1048592 | tf_op jit(solution)/shard_map/psum | solution.py:158
  433.6 2.7 maximum_bitcast_fusion
  (223 shorter events, 109.3 us)
Async XLA Ops:
  8.0 63.9 %all-reduce.4.cloned.1.call-start = ((), (), s32[]{:S(2)}) async-start(), calls=%async_computation.3 | async-start | bytes 3670016 | tf_op jit(solution)/shard_map/psum | solution.py:50
  13.4 82.9 %all-gather.10.cloned.1.call-start = ((), (), s32[]{:S(2)}) async-start(), calls=%async_computation.9 | async-start | bytes 4227072 | tf_op jit(solution)/shard_map/all_gather | solution.py:60
  14.0 111.3 %all-gather.8.cloned.1.call-start = ((), (), s32[]{:S(2)}) async-start(), calls=%async_computation.4 | async-start | bytes 4128768 | tf_op jit(solution)/shard_map/all_gather | solution.py:55
  75.8 53.4 %reduce-scatter.6.cloned.1.call-start = ((), (), s32[]{:S(2)}) async-start(), calls=%async_computation.6 | async-start | bytes 1146880 | tf_op jit(solution)/shard_map/reduce_scatter | solution.py:58
  78.2 81.5 %reduce-scatter.4.cloned.1.call-start = ((), (), s32[]{:S(2)}) async-start(), calls=%async_computation.5 | async-start | bytes 294912 | tf_op jit(solution)/shard_map/reduce_scatter | solution.py:72
  102.1 25.6 %copy-start.3 = (f32[7,128,512]{2,1,0:T(8,128)S(1)}, f32[7,128,512]{2,1,0:T(8,128)}, u32[]{:S(2)}) copy-start(f32[7,128,512]{2,1,0:T(8,128)} %copy-done.2) | copy-start | bytes 5505028
  129.1 76.9 %all-gather.12.cloned.1.call-start = ((), (), s32[]{:S(2)}) async-start(), calls=%async_computation.10 | async-start | bytes 3244032 | tf_op jit(solution)/shard_map/all_gather | solution.py:77
  161.2 96.9 %reduce-scatter.8.cloned.1.call-start = ((), (), s32[]{:S(2)}) async-start(), calls=%async_computation.7 | async-start | bytes 589824 | tf_op jit(solution)/shard_map/reduce_scatter | solution.py:72
  177.7 2.3 copy-start.13
  207.3 2.1 copy-start.7
  220.9 3.2 copy-start.15
  220.9 3.2 copy-start.16
  220.9 3.2 copy-start.20
  220.9 3.2 copy-start.36
  225.7 34.1 %copy-start.41 = (s32[1,4]{1,0:T(1,128)S(1)}, s32[1,4]{1,0:T(1,128)}, u32[]{:S(2)}) copy-start(s32[1,4]{1,0:T(1,128)} %param.15) | copy-start | bytes 52
  227.5 48.1 %copy-start.9 = (f32[1,1024,128]{2,1,0:T(8,128)S(1)}, f32[1,1024,128]{2,1,0:T(8,128)}, u32[]{:S(2)}) copy-start(f32[1,1024,128]{2,1,0:T(8,128)} %get-tuple-element.49) | copy-start | bytes 1572868
  227.5 98.9 %all-gather.14.cloned.1.call-start = ((), (), s32[]{:S(2)}) async-start(), calls=%async_computation.11 | async-start | bytes 6488064 | tf_op jit(solution)/shard_map/all_gather | solution.py:77
  259.7 173.9 %all-reduce.6.cloned.1.call-start = ((), (), s32[]{:S(2)}) async-start(), calls=%async_computation.8 | async-start | bytes 2097152 | tf_op jit(solution)/shard_map/psum | solution.py:158
  281.6 2.2 copy-start.24
  281.7 3.1 copy-start.23
  282.8 2.9 copy-start.22
  283.8 2.7 copy-start.21
  328.1 3.2 copy-start.8
  331.4 4.0 copy-start.5
  361.4 3.4 copy-start.14
  361.4 3.4 copy-start.19
  361.5 3.4 copy-start.28
  361.5 3.4 copy-start.30
  361.5 3.4 copy-start.33
  361.5 3.4 copy-start.37
  371.5 3.1 copy-start.38
  433.6 2.7 copy-start.1
  (19 other events, 29.3 us)
Sparse Core Ops, SparseCore 0:
  13.5 58.3 all-reduce.3
  79.1 22.6 reduce-scatter.5
  129.2 30.4 reduce-scatter.3
  162.1 43.8 all-gather.11
  227.6 30.4 reduce-scatter.7
  260.2 47.9 all-gather.13
Sparse Core Ops, SparseCore 1:
  17.0 79.3 all-gather.9
  98.5 26.8 all-gather.7
  372.6 60.9 all-reduce.5
where the time goes:
time: 446 us; the launch traced here: 444 us
  waiting for transfers between devices  238 us (53%)
  local copies, waits for them, and re-layouts  110 us (25%)
  other arithmetic  38.9 us (9%)
  between operations  29.3 us (7%)
  matrix products  26.3 us (6%)
    reduce_scatter x2, waiting for transfers between devices, reduce_and_gather(): lax.psum_scatter(diag_partial(first, products), 'row', scatter_dimension=...  61.1 us
    psum x1, waiting for transfers between devices, body(): diag_2 = lax.psum(diag_partial(first_2, product_2) + gram_rows, 'row')  58.1 us
    psum x1, waiting for transfers between devices, body(): factor_rows = lax.psum(partial_factor, 'col')  57.6 us
    dot_general x12, matrix products, mm(): jnp.matmul(a, b, precision=HIGHEST, preferred_element_type=jnp.float32)  26.3 us
    all_gather x2, waiting for transfers between devices, reduce_and_gather(): everything = lax.all_gather(both, ('row', 'col'), axis=0)  22.6 us
    all_gather x1, waiting for transfers between devices, body(): factor_cols = lax.all_gather(factor_tile, 'row', axis=1, tiled=True)  20.2 us
    all_gather x1, waiting for transfers between devices, body(): gathered = lax.all_gather(sigma_top, ('leaf', 'row', 'col'), axis=0)  18.1 us
    neg x8, local copies, waits for them, and re-layouts, body(): -product_row(gathered_1, parent, source_row)  14.3 us
  transfers between devices with their start and end apart: 9, of which 7 were waited for; matrix products, arithmetic and copies ran while one was open for 22% of the time, Pallas kernels for 0%

commit v1 on v0

--- a/solution.py
+++ b/solution.py
@@ -30,6 +30,12 @@
 
 
 def body(sigma_top, panels, inverse_diag, slot_lists, parent_links):
+
+    def make_widths(here_x):
+        now = lax.all_gather(here_x, "col")
+        earlier = jnp.sum(now, axis=0)
+        return earlier
+
     tile = TILE
     row_count = lax.axis_size("row")
     col_count = lax.axis_size("col")
@@ -47,7 +53,7 @@
     positions = slot_count + own_tiles
     band = width // row_count
     partial_factor = mm(panel, inverse)
-    factor_rows = lax.psum(partial_factor, "col")
+    factor_rows = make_widths(partial_factor)
     living = jnp.concatenate([jnp.ones((1, slot_count), jnp.bool_), picks_all >= 0], axis=0)
     live_here = jnp.take(living, r, axis=1).astype(jnp.float32)
     factor_rows = factor_rows * live_here[:, None, None]

time: 446 us -> 539 us (1.21)
  waiting for transfers between devices: 238 us -> 327 us
    all_gather x0 -> x1, waiting for transfers between devices: none -> 75.9 us  [make_widths(): now = lax.all_gather(here_x, 'col')]
    psum x1 -> x0, waiting for transfers between devices: 57.6 us -> none  [body(): factor_rows = lax.psum(partial_factor, 'col')]
    all_gather x1, waiting for transfers between devices: 18.1 us -> 56.6 us  [body(): gathered = lax.all_gather(sigma_top, ('leaf', 'row', 'col'), axis=0)]
    reduce_scatter x1, waiting for transfers between devices: 0.02 us -> 22.6 us  [body(): lax.psum_scatter(partial_gram, 'col', scatter_dimension=2, tiled=True)]
    reduce_sum x0 -> x1, other arithmetic: none -> 5.41 us  [make_widths(): earlier = jnp.sum(now, axis=0)]
  transfers between devices with their start and end apart: 9 -> 9, of which waited for: 7 -> 8; matrix products, arithmetic and copies ran while one was open for 22% -> 20% of each run, Pallas kernels for 0% -> 0%
where the time goes in v1:
time: 539 us; the launch traced here: 536 us
  waiting for transfers between devices  327 us (61%)
  local copies, waits for them, and re-layouts  113 us (21%)
  other arithmetic  44 us (8%)
  between operations  27 us (5%)
  matrix products  24.6 us (5%)
    all_gather x1, waiting for transfers between devices, make_widths(): now = lax.all_gather(here_x, 'col')  75.9 us
    reduce_scatter x2, waiting for transfers between devices, reduce_and_gather(): lax.psum_scatter(diag_partial(first, products), 'row', scatter_dimension=...  63.8 us
    psum x1, waiting for transfers between devices, body(): diag_2 = lax.psum(diag_partial(first_2, product_2) + gram_rows, 'row')  58.6 us
    all_gather x1, waiting for transfers between devices, body(): gathered = lax.all_gather(sigma_top, ('leaf', 'row', 'col'), axis=0)  56.6 us
    all_gather x1, waiting for transfers between devices, body(): factor_cols = lax.all_gather(factor_tile, 'row', axis=1, tiled=True)  25 us
    dot_general x12, matrix products, mm(): jnp.matmul(a, b, precision=HIGHEST, preferred_element_type=jnp.float32)  24.6 us
    all_gather x2, waiting for transfers between devices, reduce_and_gather(): everything = lax.all_gather(both, ('row', 'col'), axis=0)  24.2 us
    reduce_scatter x1, waiting for transfers between devices, body(): lax.psum_scatter(partial_gram, 'col', scatter_dimension=2, tiled=True)  22.6 us
  transfers between devices with their start and end apart: 9, of which 8 were waited for; matrix products, arithmetic and copies ran while one was open for 20% of the time, Pallas kernels for 0%

profile of v1, /device:TPU:0, one launch (start us, length us, event | category | flops | bytes accessed | tf_op | source)
XLA Modules:
  0.0 536.3 jit_solution(393394744784764036)
XLA Ops:
  8.7 3.9 fusion.2
  13.7 75.9 %all-gather.14.cloned.1.call-done = f32[28,128,512]{2,1,0:T(8,128)} async-done(((f32[7,128,512]{2,1,0:T(8,128)}), f32[28,128,512]{2,1,0:T(8,128)}) %all-gather.14.cloned.1.call-update) | async-done | bytes 7340048 | tf_op jit(solution)/shard_map/all_gather | solution.py:35
  89.6 5.4 %reduce_sum.9 = f32[7,128,512]{2,1,0:T(8,128)} reduce(f32[4,7,128,512]{3,2,1,0:T(8,128)} %bitcast.298, f32[]{:T(128)} %constant.521.clone.1), dimensions={0}, to_apply=%region_0.0 | reduce | flops 1376256 | bytes 9175044 | tf_op jit(solution)/shard_map/reduce_sum | solution.py:36
  95.0 2.8 copy.204
  101.5 2.2 fusion
  103.8 56.6 %all-gather.12.cloned.1.call-done = f32[4096,256]{1,0:T(8,128)} async-done(((f32[32,256]{1,0:T(8,128)}), f32[4096,256]{1,0:T(8,128)}) %all-gather.12.cloned.1.call-update) | async-done | bytes 4194320 | tf_op jit(solution)/shard_map/all_gather | solution.py:66
  160.4 5.8 %copy.203 = f32[32,4,32,256]{3,1,2,0:T(4,128)S(1)} copy(f32[32,4,32,256]{3,2,1,0:T(8,128)} %bitcast.301) | data formatting | bytes 8388608 | tf_op jit(solution)/shard_map/reshape | solution.py:67
  166.2 3.1 copy.263
  169.3 25.0 %all-gather.10.cloned.1.call-done = f32[7,1024,128]{1,2,0:T(8,128)} async-done(((f32[7,128,128]{1,2,0:T(8,128)}), f32[7,1024,128]{1,2,0:T(8,128)}) %all-gather.10.cloned.1.call-update) | async-done | bytes 3670032 | tf_op jit(solution)/shard_map/all_gather | solution.py:61
  194.3 2.4 bitcast_dynamic-update-slice_fusion.6
  197.8 22.6 %reduce-scatter.6.cloned.1.call-done = f32[7,64,128]{2,1,0:T(8,128)} async-done(((f32[7,64,512]{2,1,0:T(8,128)}), f32[7,64,128]{2,1,0:T(8,128)}) %reduce-scatter.6.cloned.1.call-update) | async-done | bytes 229392 | tf_op jit(solution)/shard_map/reduce_scatter | solution.py:64
  220.4 33.3 %reduce-scatter.4.cloned.1.call-done = f32[1,64,128]{2,1,0:T(8,128)} async-done(((f32[1,512,128]{2,1,0:T(8,128)}), f32[1,64,128]{2,1,0:T(8,128)}) %reduce-scatter.4.cloned.1.call-update) | async-done | bytes 32784 | tf_op jit(solution)/shard_map/reduce_scatter | solution.py:78
  264.3 2.3 constant_dynamic-slice_fusion.14
  266.6 3.4 fusion.109
  272.5 2.2 select_select_fusion.4
  275.7 24.2 %all-gather.16.cloned.1.call-done = f32[32,192,128]{2,1,0:T(8,128)} async-done(((f32[1,192,128]{2,1,0:T(8,128)}), f32[32,192,128]{2,1,0:T(8,128)}) %all-gather.16.cloned.1.call-update) | async-done | bytes 3145744 | tf_op jit(solution)/shard_map/all_gather | solution.py:83
  301.2 2.1 slice.193
  308.3 3.3 constant_dynamic-slice_fusion.6
  312.9 3.0 bitcast_dynamic-update-slice_fusion.5
  318.9 30.5 %reduce-scatter.8.cloned.1.call-done = f32[2,64,128]{2,1,0:T(8,128)} async-done(((f32[2,512,128]{2,1,0:T(8,128)}), f32[2,64,128]{2,1,0:T(8,128)}) %reduce-scatter.8.cloned.1.call-update) | async-done | bytes 65552 | tf_op jit(solution)/shard_map/reduce_scatter | solution.py:78
  366.6 2.6 gather_fusion.9
  383.2 2.3 gather_fusion.8
  393.0 2.3 gather_fusion.6
  402.7 2.3 gather_fusion.4
  412.4 2.3 gather_fusion.2
  421.8 3.2 slice.198
  434.5 2.3 negate_bitcast_fusion
  451.1 2.1 copy.256
  453.1 2.1 copy.254
  455.2 3.3 bitcast_dynamic-update-slice_fusion.3
  468.5 58.6 %all-reduce.3.cloned.1.call-done = f32[4,512,128]{2,1,0:T(8,128)} async-done(((f32[4,512,128]{2,1,0:T(8,128)}), f32[4,512,128]{2,1,0:T(8,128)}) %all-reduce.3.cloned.1.call-update) | async-done | bytes 1048592 | tf_op jit(solution)/shard_map/psum | solution.py:164
  527.1 2.7 maximum_bitcast_fusion
  (231 shorter events, 113.4 us)
Async XLA Ops:
  7.2 82.4 %all-gather.14.cloned.1.call-start = ((), (), s32[]{:S(2)}) async-start(), calls=%async_computation.9 | async-start | bytes 9175040 | tf_op jit(solution)/shard_map/all_gather | solution.py:35
  12.6 147.9 %all-gather.12.cloned.1.call-start = ((), (), s32[]{:S(2)}) async-start(), calls=%async_computation.8 | async-start | bytes 4227072 | tf_op jit(solution)/shard_map/all_gather | solution.py:66
  13.3 181.0 %all-gather.10.cloned.1.call-start = ((), (), s32[]{:S(2)}) async-start(), calls=%async_computation.3 | async-start | bytes 4128768 | tf_op jit(solution)/shard_map/all_gather | solution.py:61
  101.5 118.9 %reduce-scatter.6.cloned.1.call-start = ((), (), s32[]{:S(2)}) async-start(), calls=%async_computation.5 | async-start | bytes 1146880 | tf_op jit(solution)/shard_map/reduce_scatter | solution.py:64
  103.8 149.9 %reduce-scatter.4.cloned.1.call-start = ((), (), s32[]{:S(2)}) async-start(), calls=%async_computation.4 | async-start | bytes 294912 | tf_op jit(solution)/shard_map/reduce_scatter | solution.py:78
  166.2 30.5 %copy-start.3 = (f32[7,128,512]{1,2,0:T(8,128)S(1)}, f32[7,128,512]{1,2,0:T(8,128)}, u32[]{:S(2)}) copy-start(f32[7,128,512]{1,2,0:T(8,128)} %copy-done.2) | copy-start | bytes 5505028
  197.8 102.1 %all-gather.16.cloned.1.call-start = ((), (), s32[]{:S(2)}) async-start(), calls=%async_computation.10 | async-start | bytes 3244032 | tf_op jit(solution)/shard_map/all_gather | solution.py:83
  255.1 94.2 %reduce-scatter.8.cloned.1.call-start = ((), (), s32[]{:S(2)}) async-start(), calls=%async_computation.6 | async-start | bytes 589824 | tf_op jit(solution)/shard_map/reduce_scatter | solution.py:78
  301.2 2.1 copy-start.7
  311.5 4.3 copy-start.13
  312.8 3.0 copy-start.20
  312.8 3.0 copy-start.36
  317.4 33.6 %copy-start.41 = (s32[1,4]{1,0:T(1,128)S(1)}, s32[1,4]{1,0:T(1,128)}, u32[]{:S(2)}) copy-start(s32[1,4]{1,0:T(1,128)} %param.15) | copy-start | bytes 52
  317.4 46.5 %copy-start.16 = (f32[1,1024,128]{1,2,0:T(8,128)S(1)}, f32[1,1024,128]{1,2,0:T(8,128)}, u32[]{:S(2)}) copy-start(f32[1,1024,128]{1,2,0:T(8,128)} %get-tuple-element.49) | copy-start | bytes 1572868
  317.4 47.5 %copy-start.15 = (f32[1,1024,128]{1,2,0:T(8,128)S(1)}, f32[1,1024,128]{1,2,0:T(8,128)}, u32[]{:S(2)}) copy-start(f32[1,1024,128]{1,2,0:T(8,128)} %get-tuple-element.50) | copy-start | bytes 1572868
  318.8 46.3 %copy-start.14 = (f32[1,1024,128]{1,2,0:T(8,128)S(1)}, f32[1,1024,128]{1,2,0:T(8,128)}, u32[]{:S(2)}) copy-start(f32[1,1024,128]{1,2,0:T(8,128)} %get-tuple-element.51) | copy-start | bytes 1572868
  318.8 101.2 %all-gather.18.cloned.1.call-start = ((), (), s32[]{:S(2)}) async-start(), calls=%async_computation.11 | async-start | bytes 6488064 | tf_op jit(solution)/shard_map/all_gather | solution.py:83
  350.9 176.1 %all-reduce.3.cloned.1.call-start = ((), (), s32[]{:S(2)}) async-start(), calls=%async_computation.7 | async-start | bytes 2097152 | tf_op jit(solution)/shard_map/psum | solution.py:164
  375.3 2.2 copy-start.24
  375.3 3.1 copy-start.23
  376.5 2.9 copy-start.22
  377.5 2.7 copy-start.21
  421.8 3.2 copy-start.8
  425.1 4.0 copy-start.5
  455.2 3.4 copy-start.12
  455.2 3.4 copy-start.19
  455.2 3.4 copy-start.28
  455.2 3.4 copy-start.30
  455.2 3.4 copy-start.33
  455.2 3.4 copy-start.37
  464.5 3.1 copy-start.38
  527.1 2.7 copy-start.1
  (19 other events, 28.3 us)
Sparse Core Ops, SparseCore 0:
  12.7 76.8 all-gather.13
  92.7 67.6 all-gather.11
  162.7 31.5 all-gather.9
  196.6 23.7 reduce-scatter.5
  223.2 30.4 reduce-scatter.3
  256.0 43.8 all-gather.15
  319.0 30.3 reduce-scatter.7
  351.6 47.9 all-gather.17
  465.6 61.3 all-reduce.2
